TPU v7x, 128 devices: a whole 4x4x4 slice. The times are simulated.
128 devices in a mesh: grp: 4 (over z_lo, core), mem: 32 (over z_hi, x, y).
Axes of the slice: x: 4, y: 4, z: 4 (z_hi: 2, z_lo: 2; z = z_hi * 2 + z_lo), core: 2. Of those that a mesh axis runs over, the one named last changes fastest.
Arguments:
- source_pts: float32 [64, 32768], P(None, ('grp', 'mem')), may hold values from -30 to 30
- target_pts: float32 [64, 32768], P(None, ('grp', 'mem')), may hold values from -30 to 30
- source_pot: float32 [32768], P(('grp', 'mem')), may hold values from -8 to 520
- target_pot: float32 [32768], P(('grp', 'mem')), may hold values from -8 to 520
- source_logw: float32 [32768], P(('grp', 'mem')), may hold values from -1 to 4
- target_logw: float32 [32768], P(('grp', 'mem')), may hold values from -1 to 4
Outputs:
- source_new: float32 [32768], P(('grp', 'mem'))
- target_new: float32 [32768], P(('grp', 'mem'))
All inputs are finite; a program needn't handle non-finite values.
Results may differ from a plain program's by a relative error of at most 0.0001.
Values sent between devices are 32-bit elements; how exact they have to be, the bound alone decides.
No kernel may reach another device: no remote copies, remote signals or barrier semaphores. Data moves between devices by JAX's collectives and lax.ppermute only.
A program may use at most 64 MiB of HBM per device.

v0:
```python
import math
import jax
import jax.numpy as jnp
from jax import lax
from jax.sharding import Mesh
from jax.sharding import PartitionSpec as P

GRP_MEM = ("grp_0", "grp_1", "mem_0", "mem_1", "mem_2")
MEM = ("mem_0", "mem_1", "mem_2")
GRP = ("grp_0", "grp_1")
epsilon = 4.0
floor_value = -1e30


def by_axis(x, axes):
    for axis in axes:
        x = lax.pmax(x, axis)
    return x


def by_axis_2(x, axes):
    for axis in axes:
        x = lax.psum(x, axis)
    return x


def in_order(pieces, dim):
    dims = list(pieces.shape[1:])
    dims[dim] *= pieces.shape[0]
    return jnp.moveaxis(pieces, 0, dim).reshape(dims)


def sent_to_all(x, axis):
    copies = jnp.broadcast_to(x, (lax.axis_size(axis), *x.shape))
    return lax.all_to_all(copies, axis, split_axis=0, concat_axis=0, tiled=True)


def collect(x, axis, dim):
    return in_order(sent_to_all(x, axis), dim)


def over_copies(x, axis):
    return sent_to_all(x, axis).max(axis=0)


def cut_along(x, dim, devices):
    dims = x.shape
    pieces = x.reshape(*dims[:dim], devices, dims[dim] // devices, *dims[dim + 1 :])
    return jnp.moveaxis(pieces, dim, 0)


def sum_at_owner(x, axis, dim):
    devices = lax.axis_size(axis)
    pieces = lax.all_to_all(cut_along(x, dim, devices), axis, 0, 0, tiled=True)
    return jnp.sum(pieces, axis=0)


def sweep(carry, points, squares, row_term, moving, offset):
    count = moving.shape[1]
    limit = 128
    width = math.gcd(count, limit)

    def block(index, state):
        row_max, row_sum, col_max, col_sum = state
        begin = index * width
        cols = lax.dynamic_slice_in_dim(moving, begin, width, 1)
        ycols = cols[:-1]
        cvals = cols[-1]
        ysq = 0.5 * jnp.sum(ycols * ycols, 0)
        cross = lax.dot_general(
            points,
            ycols,
            (((0,), (0,)), ((), ())),
            precision=lax.Precision.HIGHEST,
            preferred_element_type=jnp.float32,
        )
        half = (squares[:, None] + ysq[None, :] - cross) / epsilon
        scores = cvals[None, :] - half
        new_row = jnp.maximum(row_max, jnp.max(scores, 1))
        row_sum = row_sum * jnp.exp(row_max - new_row) + jnp.sum(
            jnp.exp(scores - new_row[:, None]), 1
        )
        others = row_term[:, None] - half
        place = offset + begin
        old_max = lax.dynamic_slice_in_dim(col_max, place, width, 0)
        old_sum = lax.dynamic_slice_in_dim(col_sum, place, width, 0)
        new_col = jnp.maximum(old_max, jnp.max(others, 0))
        new_sum = old_sum * jnp.exp(old_max - new_col) + jnp.sum(
            jnp.exp(others - new_col[None, :]), 0
        )
        col_max = lax.dynamic_update_slice_in_dim(col_max, new_col, place, 0)
        col_sum = lax.dynamic_update_slice_in_dim(col_sum, new_sum, place, 0)
        return (new_row, row_sum, col_max, col_sum)

    return lax.fori_loop(0, count // width, block, carry)


def totals(source_logw, target_logw):
    peaks = (by_axis(jnp.max(source_logw), GRP_MEM), by_axis(jnp.max(target_logw), GRP_MEM))
    masses = (
        by_axis_2(jnp.sum(jnp.exp(source_logw - peaks[0])), GRP_MEM),
        by_axis_2(jnp.sum(jnp.exp(target_logw - peaks[1])), GRP_MEM),
    )
    return (peaks[0] + jnp.log(masses[0]), peaks[1] + jnp.log(masses[1]))


def local(source_pts, target_pts, source_pot, target_pot, source_logw, target_logw):
    members = lax.axis_size(MEM)
    rows = source_pts.shape[1]
    outer = rows * members
    row_term = source_logw + source_pot / epsilon
    col_term = target_logw + target_pot / epsilon
    moving = jnp.concatenate([target_pts, col_term[None, :]], 0)
    standing = jnp.concatenate([source_pts, row_term[None, :]], 0)
    row_block = collect(standing, MEM, 1)
    col_block = collect(moving, GRP, 1)
    block_pts = row_block[:-1]
    block_terms = row_block[-1]
    block_sq = 0.5 * jnp.sum(block_pts * block_pts, 0)
    span = col_block.shape[1]
    carry = (
        jnp.full((outer,), floor_value, jnp.float32),
        jnp.zeros((outer,), jnp.float32),
        jnp.full((span,), floor_value, jnp.float32),
        jnp.zeros((span,), jnp.float32),
    )
    row_max, row_sum, col_max, col_sum = sweep(
        carry, block_pts, block_sq, block_terms, col_block, 0
    )
    rpeak = over_copies(row_max, MEM)
    own_rsum = sum_at_owner(row_sum * jnp.exp(row_max - rpeak), MEM, 0)
    own_rmax = lax.dynamic_slice_in_dim(rpeak, lax.axis_index(MEM) * rows, rows, 0)
    row_total = own_rmax + jnp.log(own_rsum)
    cpeak = over_copies(col_max, GRP)
    own_sum = sum_at_owner(col_sum * jnp.exp(col_max - cpeak), GRP, 0)
    own_max = lax.dynamic_slice_in_dim(cpeak, lax.axis_index(GRP) * rows, rows, 0)
    col_total = own_max + jnp.log(own_sum)
    src_norm, tgt_norm = totals(source_logw, target_logw)
    row_hat = -epsilon * (row_total - tgt_norm)
    col_hat = -epsilon * (col_total - src_norm)
    return (0.5 * (source_pot + row_hat), 0.5 * (target_pot + col_hat))


def solution(mesh):
    finer = Mesh(mesh.devices.reshape(2, 2, 2, 4, 4), ("grp_0", "grp_1", "mem_0", "mem_1", "mem_2"))
    return jax.shard_map(
        local,
        mesh=finer,
        in_specs=(
            P(None, GRP_MEM),
            P(None, GRP_MEM),
            P(GRP_MEM),
            P(GRP_MEM),
            P(GRP_MEM),
            P(GRP_MEM),
        ),
        out_specs=(P(GRP_MEM), P(GRP_MEM)),
        check_vma=False,
    )
```

profile of v0, /device:TPU:0, one launch (start us, length us, event | category | flops | bytes accessed | tf_op | source)
XLA Modules:
  0.0 235.5 jit_solution(10569163708637977095)
XLA Ops:
  0.6 1.3 reduce_max.63
  1.9 1.3 reduce_max.65
  3.2 5.6 %all-reduce.9 = (f32[]{:T(128)}, f32[]{:T(128)}) all-reduce(f32[]{:T(128)} %reduce_max.63, f32[]{:T(128)} %reduce_max.65), channel_id=1, replica_groups=mesh['grp_0'=2,'grp_1'=2,'mem_0'=2,'mem_1'=4,'mem_2'=4] {'grp_0'}, use_global_device_ids=true, to_apply=%region_11.0 | all-reduce | flops 2 | bytes 16 | tf_op jit(solution)/shard_map/pmax | solution.py:17
  8.8 3.1 %all-reduce.8 = (f32[]{:T(128)}, f32[]{:T(128)}) all-reduce(f32[]{:T(128)} %get-tuple-element.233, f32[]{:T(128)} %get-tuple-element.234), channel_id=1, replica_groups=mesh['grp_0'=2,'grp_1'=2,'mem_0'=2,'mem_1'=4,'mem_2'=4] {'grp_1'}, use_global_device_ids=true, to_apply=%region_12.0 | all-reduce | flops 2 | bytes 16 | tf_op jit(solution)/shard_map/pmax | solution.py:17
  11.8 7.5 %all-reduce.7 = (f32[]{:T(128)}, f32[]{:T(128)}) all-reduce(f32[]{:T(128)} %get-tuple-element.231, f32[]{:T(128)} %get-tuple-element.232), channel_id=1, replica_groups=mesh['grp_0'=2,'grp_1'=2,'mem_0'=2,'mem_1'=4,'mem_2'=4] {'mem_0'}, use_global_device_ids=true, to_apply=%region_13.0 | all-reduce | flops 2 | bytes 16 | tf_op jit(solution)/shard_map/pmax | solution.py:17
  19.3 11.1 %all-reduce.3 = (f32[]{:T(128)}, f32[]{:T(128)}) all-reduce(f32[]{:T(128)} %get-tuple-element.229, f32[]{:T(128)} %get-tuple-element.230), channel_id=1, replica_groups=mesh['grp_0'=2,'grp_1'=2,'mem_0'=2,'mem_1'=4,'mem_2'=4] {'mem_1'}, use_global_device_ids=true, to_apply=%region_14.0 | all-reduce | flops 2 | bytes 16 | tf_op jit(solution)/shard_map/pmax | solution.py:17
  30.4 11.4 %all-reduce.2 = (f32[]{:T(128)}, f32[]{:T(128)}) all-reduce(f32[]{:T(128)} %get-tuple-element.221, f32[]{:T(128)} %get-tuple-element.222), channel_id=1, replica_groups=mesh['grp_0'=2,'grp_1'=2,'mem_0'=2,'mem_1'=4,'mem_2'=4] {'mem_2'}, use_global_device_ids=true, to_apply=%region_15.0 | all-reduce | flops 2 | bytes 16 | tf_op jit(solution)/shard_map/pmax | solution.py:17
  41.8 2.6 %exponential_reduce_fusion.2 = (f32[]{:T(128)}, f32[256]{0:T(256)S(1)}, f32[256]{0:T(256)S(1)}, f32[]{:T(128)}) fusion(f32[256]{0:T(256)} %param.12, f32[]{:T(128)} %get-tuple-element.220, f32[256]{0:T(256)} %param.10, f32[256]{0:T(256)} %param.13, f32[256]{0:T(256)} %param.11, f32[]{:T(128)} %get-tuple-element.219), kind=kLoop, calls=%fused_computation.25 | loop fusion | flops 2046 | bytes 6160 | tf_op jit(solution)/shard_map/reduce_sum | solution.py:101
  44.4 0.8 pad_maximum_fusion
  45.2 0.7 broadcast_in_dim.47
  46.0 3.5 %all-to-all-start = ((f32[4,65,256]{2,1,0:T(8,128)}), f32[4,65,256]{2,1,0:T(8,128)S(1)}, u32[]{:S(2)}, u32[]{:S(2)}) async-start(f32[4,65,256]{2,1,0:T(8,128)} %broadcast_in_dim.47), calls=%async_computation | async-start | bytes 589824 | tf_op jit(solution)/shard_map/all_to_all | solution.py:35
  49.4 0.8 pad_maximum_fusion.1
  50.3 5.5 %all-to-all-done = f32[4,65,256]{2,1,0:T(8,128)S(1)} async-done(((f32[4,65,256]{2,1,0:T(8,128)}), f32[4,65,256]{2,1,0:T(8,128)S(1)}, u32[]{:S(2)}, u32[]{:S(2)}) %all-to-all-start) | async-done | bytes 266272 | tf_op jit(solution)/shard_map/all_to_all | solution.py:35
  55.8 1.6 broadcast_in_dim.49
  57.3 5.8 %all-to-all-start.1 = ((f32[32,65,256]{2,1,0:T(8,128)}), f32[32,65,256]{2,1,0:T(8,128)S(1)}, u32[]{:S(2)}, u32[]{:S(2)}) async-start(f32[32,65,256]{2,1,0:T(8,128)} %broadcast_in_dim.49), calls=%async_computation.1 | async-start | bytes 4718592 | tf_op jit(solution)/shard_map/all_to_all | solution.py:35
  63.4 31.0 %all-to-all-done.1 = f32[32,65,256]{2,1,0:T(8,128)S(1)} async-done(((f32[32,65,256]{2,1,0:T(8,128)}), f32[32,65,256]{2,1,0:T(8,128)S(1)}, u32[]{:S(2)}, u32[]{:S(2)}) %all-to-all-start.1) | async-done | bytes 2129952 | tf_op jit(solution)/shard_map/all_to_all | solution.py:35
  94.4 0.4 slice_bitcast_fusion
  95.1 53.8 %while.20 = (s32[]{:T(128)}, f32[8192]{0:T(1024)S(1)}, f32[8192]{0:T(1024)S(1)}, f32[1024]{0:T(1024)S(1)}, f32[1024]{0:T(1024)S(1)}, /*index=5*/f32[65,1024]{1,0...) while((s32[]{:T(128)}, f32[8192]{0:T(1024)S(1)}, ...), condition=%wide.region_7.0_spmd.clone, body=%wide.region_1.0_spmd.clone.sunk | while | flops 818995456 | bytes 11102442 | solution.py:95
  95.2 4.5 %subtract_reduce_fusion.3 = (f32[128]{0:T(128)S(1)}, f32[8192]{0:T(1024)S(1)}, f32[8192,128]{0,1:T(8,128)S(1)}) fusion(f32[8192]{0:T(1024)S(1)} %bitcast.36, f32[128]{0:T(128)S(1)} %dynamic-slice_bitcast_fusion.2, f32[64,8192]{1,0:T(8,128)S(1)} %get-tuple-element.350, f32[65,1024]{1,0:T(8,128)S(1)} %get-tuple-element.348, s32[]{:T(128)S(6)} %select_n.21, ...), kind=kOutput, calls=%fused_computation.5.clone.1 | convolution fusion | flops 812638080 | bytes 6424068 | tf_op jit(solution)/shard_map/while/body/eval_jaxpr/dot_general | solution.py:70
  99.7 0.2 fusion.11
  99.9 1.7 exponential_reduce_fusion.5
  101.7 0.2 add_dynamic-update-slice_fusion.2
  101.9 4.5 %subtract_reduce_fusion.3 = (f32[128]{0:T(128)S(1)}, f32[8192]{0:T(1024)S(1)}, f32[8192,128]{0,1:T(8,128)S(1)}) fusion(f32[8192]{0:T(1024)S(1)} %bitcast.36, f32[128]{0:T(128)S(1)} %dynamic-slice_bitcast_fusion.2, f32[64,8192]{1,0:T(8,128)S(1)} %get-tuple-element.350, f32[65,1024]{1,0:T(8,128)S(1)} %get-tuple-element.348, s32[]{:T(128)S(6)} %select_n.21, ...), kind=kOutput, calls=%fused_computation.5.clone.1 | convolution fusion | flops 812638080 | bytes 6424068 | tf_op jit(solution)/shard_map/while/body/eval_jaxpr/dot_general | solution.py:70
  106.5 0.2 fusion.11
  106.6 1.7 exponential_reduce_fusion.5
  108.4 0.2 add_dynamic-update-slice_fusion.2
  108.6 4.5 %subtract_reduce_fusion.3 = (f32[128]{0:T(128)S(1)}, f32[8192]{0:T(1024)S(1)}, f32[8192,128]{0,1:T(8,128)S(1)}) fusion(f32[8192]{0:T(1024)S(1)} %bitcast.36, f32[128]{0:T(128)S(1)} %dynamic-slice_bitcast_fusion.2, f32[64,8192]{1,0:T(8,128)S(1)} %get-tuple-element.350, f32[65,1024]{1,0:T(8,128)S(1)} %get-tuple-element.348, s32[]{:T(128)S(6)} %select_n.21, ...), kind=kOutput, calls=%fused_computation.5.clone.1 | convolution fusion | flops 812638080 | bytes 6424068 | tf_op jit(solution)/shard_map/while/body/eval_jaxpr/dot_general | solution.py:70
  113.2 0.2 fusion.11
  113.4 1.7 exponential_reduce_fusion.5
  115.1 0.2 add_dynamic-update-slice_fusion.2
  115.3 4.5 %subtract_reduce_fusion.3 = (f32[128]{0:T(128)S(1)}, f32[8192]{0:T(1024)S(1)}, f32[8192,128]{0,1:T(8,128)S(1)}) fusion(f32[8192]{0:T(1024)S(1)} %bitcast.36, f32[128]{0:T(128)S(1)} %dynamic-slice_bitcast_fusion.2, f32[64,8192]{1,0:T(8,128)S(1)} %get-tuple-element.350, f32[65,1024]{1,0:T(8,128)S(1)} %get-tuple-element.348, s32[]{:T(128)S(6)} %select_n.21, ...), kind=kOutput, calls=%fused_computation.5.clone.1 | convolution fusion | flops 812638080 | bytes 6424068 | tf_op jit(solution)/shard_map/while/body/eval_jaxpr/dot_general | solution.py:70
  119.9 0.2 fusion.11
  120.1 1.7 exponential_reduce_fusion.5
  121.8 0.2 add_dynamic-update-slice_fusion.2
  122.1 4.5 %subtract_reduce_fusion.3 = (f32[128]{0:T(128)S(1)}, f32[8192]{0:T(1024)S(1)}, f32[8192,128]{0,1:T(8,128)S(1)}) fusion(f32[8192]{0:T(1024)S(1)} %bitcast.36, f32[128]{0:T(128)S(1)} %dynamic-slice_bitcast_fusion.2, f32[64,8192]{1,0:T(8,128)S(1)} %get-tuple-element.350, f32[65,1024]{1,0:T(8,128)S(1)} %get-tuple-element.348, s32[]{:T(128)S(6)} %select_n.21, ...), kind=kOutput, calls=%fused_computation.5.clone.1 | convolution fusion | flops 812638080 | bytes 6424068 | tf_op jit(solution)/shard_map/while/body/eval_jaxpr/dot_general | solution.py:70
  126.6 0.2 fusion.11
  126.8 1.7 exponential_reduce_fusion.5
  128.5 0.2 add_dynamic-update-slice_fusion.2
  128.8 4.5 %subtract_reduce_fusion.3 = (f32[128]{0:T(128)S(1)}, f32[8192]{0:T(1024)S(1)}, f32[8192,128]{0,1:T(8,128)S(1)}) fusion(f32[8192]{0:T(1024)S(1)} %bitcast.36, f32[128]{0:T(128)S(1)} %dynamic-slice_bitcast_fusion.2, f32[64,8192]{1,0:T(8,128)S(1)} %get-tuple-element.350, f32[65,1024]{1,0:T(8,128)S(1)} %get-tuple-element.348, s32[]{:T(128)S(6)} %select_n.21, ...), kind=kOutput, calls=%fused_computation.5.clone.1 | convolution fusion | flops 812638080 | bytes 6424068 | tf_op jit(solution)/shard_map/while/body/eval_jaxpr/dot_general | solution.py:70
  133.3 0.2 fusion.11
  133.5 1.7 exponential_reduce_fusion.5
  135.3 0.2 add_dynamic-update-slice_fusion.2
  135.5 4.5 %subtract_reduce_fusion.3 = (f32[128]{0:T(128)S(1)}, f32[8192]{0:T(1024)S(1)}, f32[8192,128]{0,1:T(8,128)S(1)}) fusion(f32[8192]{0:T(1024)S(1)} %bitcast.36, f32[128]{0:T(128)S(1)} %dynamic-slice_bitcast_fusion.2, f32[64,8192]{1,0:T(8,128)S(1)} %get-tuple-element.350, f32[65,1024]{1,0:T(8,128)S(1)} %get-tuple-element.348, s32[]{:T(128)S(6)} %select_n.21, ...), kind=kOutput, calls=%fused_computation.5.clone.1 | convolution fusion | flops 812638080 | bytes 6424068 | tf_op jit(solution)/shard_map/while/body/eval_jaxpr/dot_general | solution.py:70
  140.1 0.2 fusion.11
  140.3 1.7 exponential_reduce_fusion.5
  142.0 0.2 add_dynamic-update-slice_fusion.2
  142.2 4.5 %subtract_reduce_fusion.3 = (f32[128]{0:T(128)S(1)}, f32[8192]{0:T(1024)S(1)}, f32[8192,128]{0,1:T(8,128)S(1)}) fusion(f32[8192]{0:T(1024)S(1)} %bitcast.36, f32[128]{0:T(128)S(1)} %dynamic-slice_bitcast_fusion.2, f32[64,8192]{1,0:T(8,128)S(1)} %get-tuple-element.350, f32[65,1024]{1,0:T(8,128)S(1)} %get-tuple-element.348, s32[]{:T(128)S(6)} %select_n.21, ...), kind=kOutput, calls=%fused_computation.5.clone.1 | convolution fusion | flops 812638080 | bytes 6424068 | tf_op jit(solution)/shard_map/while/body/eval_jaxpr/dot_general | solution.py:70
  147.0 1.7 exponential_reduce_fusion.5
  148.7 0.2 add_dynamic-update-slice_fusion.2
  148.9 6.2 %all_to_all.40 = f32[4,1,1024]{2,1,0:T(1,128)S(1)} all-to-all(f32[4,1,1024]{2,1,0:T(1,128)S(1)} %broadcast_in_dim.51), channel_id=1, replica_groups=mesh['grp_0'=2,'grp_1'=2,'mem_0'=2,'mem_1'=4,'mem_2'=4] {'grp_0','grp_1'}, dimensions={0} | all-to-all | bytes 32768 | tf_op jit(solution)/shard_map/all_to_all | solution.py:35
  155.2 6.1 %all_to_all.41 = f32[4,1,256]{2,1,0:T(1,128)S(1)} all-to-all(f32[4,1,256]{2,1,0:T(1,128)S(1)} %bitcast.42), channel_id=1, replica_groups=mesh['grp_0'=2,'grp_1'=2,'mem_0'=2,'mem_1'=4,'mem_2'=4] {'grp_0','grp_1'}, dimensions={0} | all-to-all | bytes 8192 | tf_op jit(solution)/shard_map/all_to_all | solution.py:54
  161.3 1.9 broadcast_in_dim.50
  163.2 7.4 %all-to-all-start.2 = ((f32[32,1,8192]{2,1,0:T(1,128)}), f32[32,1,8192]{2,1,0:T(1,128)S(1)}, u32[]{:S(2)}, u32[]{:S(2)}) async-start(f32[32,1,8192]{2,1,0:T(1,128)} %broadcast_in_dim.50), calls=%async_computation.2 | async-start | bytes 2097152 | tf_op jit(solution)/shard_map/all_to_all | solution.py:35
  170.7 5.5 %all-reduce.6 = (f32[]{:T(128)}, f32[]{:T(128)}) all-reduce(f32[]{:T(128)} %get-tuple-element.245, f32[]{:T(128)} %get-tuple-element.240), channel_id=1, replica_groups=mesh['grp_0'=2,'grp_1'=2,'mem_0'=2,'mem_1'=4,'mem_2'=4] {'grp_0'}, use_global_device_ids=true, to_apply=%region_17.0 | all-reduce | flops 2 | bytes 16 | tf_op jit(solution)/shard_map/psum | solution.py:23
  176.2 3.1 %all-reduce.5 = (f32[]{:T(128)}, f32[]{:T(128)}) all-reduce(f32[]{:T(128)} %get-tuple-element.227, f32[]{:T(128)} %get-tuple-element.228), channel_id=1, replica_groups=mesh['grp_0'=2,'grp_1'=2,'mem_0'=2,'mem_1'=4,'mem_2'=4] {'grp_1'}, use_global_device_ids=true, to_apply=%region_18.0 | all-reduce | flops 2 | bytes 16 | tf_op jit(solution)/shard_map/psum | solution.py:23
  179.3 7.3 %all-reduce.4 = (f32[]{:T(128)}, f32[]{:T(128)}) all-reduce(f32[]{:T(128)} %get-tuple-element.225, f32[]{:T(128)} %get-tuple-element.226), channel_id=1, replica_groups=mesh['grp_0'=2,'grp_1'=2,'mem_0'=2,'mem_1'=4,'mem_2'=4] {'mem_0'}, use_global_device_ids=true, to_apply=%region_19.0 | all-reduce | flops 2 | bytes 16 | tf_op jit(solution)/shard_map/psum | solution.py:23
  186.6 15.7 %all-reduce.1 = (f32[]{:T(128)}, f32[]{:T(128)}) all-reduce(f32[]{:T(128)} %get-tuple-element.223, f32[]{:T(128)} %get-tuple-element.224), channel_id=1, replica_groups=mesh['grp_0'=2,'grp_1'=2,'mem_0'=2,'mem_1'=4,'mem_2'=4] {'mem_1'}, use_global_device_ids=true, to_apply=%region_20.0 | all-reduce | flops 2 | bytes 16 | tf_op jit(solution)/shard_map/psum | solution.py:23
  202.3 12.9 %all-reduce = (f32[]{:T(128)}, f32[]{:T(128)}) all-reduce(f32[]{:T(128)} %get-tuple-element.217, f32[]{:T(128)} %get-tuple-element.218), channel_id=1, replica_groups=mesh['grp_0'=2,'grp_1'=2,'mem_0'=2,'mem_1'=4,'mem_2'=4] {'mem_2'}, use_global_device_ids=true, to_apply=%region_21.0 | all-reduce | flops 2 | bytes 16 | tf_op jit(solution)/shard_map/psum | solution.py:23
  217.8 0.7 reduce_max.62
  218.5 0.6 exponential_multiply_fusion
  219.1 5.8 %all-to-all-start.3 = ((f32[32,1,256]{2,1,0:T(1,128)}), f32[32,1,256]{2,1,0:T(1,128)S(1)}, u32[]{:S(2)}, u32[]{:S(2)}) async-start(f32[32,1,256]{2,1,0:T(1,128)} %bitcast.5), calls=%async_computation.3 | async-start | bytes 65536 | tf_op jit(solution)/shard_map/all_to_all | solution.py:54
  224.9 0.6 add_multiply_fusion
  225.6 9.2 %all-to-all-done.3 = f32[32,1,256]{2,1,0:T(1,128)S(1)} async-done(((f32[32,1,256]{2,1,0:T(1,128)}), f32[32,1,256]{2,1,0:T(1,128)S(1)}, u32[]{:S(2)}, u32[]{:S(2)}) %all-to-all-start.3) | async-done | bytes 32800 | tf_op jit(solution)/shard_map/all_to_all | solution.py:54
  234.8 0.6 add_multiply_fusion.1
  (86 shorter events, 1.3 us)
Async XLA Ops:
  46.0 9.8 %all-to-all-start = ((f32[4,65,256]{2,1,0:T(8,128)}), f32[4,65,256]{2,1,0:T(8,128)S(1)}, u32[]{:S(2)}, u32[]{:S(2)}) async-start(f32[4,65,256]{2,1,0:T(8,128)} %broadcast_in_dim.47), calls=%async_computation | async-start | bytes 589824 | tf_op jit(solution)/shard_map/all_to_all | solution.py:35
  57.3 37.1 %all-to-all-start.1 = ((f32[32,65,256]{2,1,0:T(8,128)}), f32[32,65,256]{2,1,0:T(8,128)S(1)}, u32[]{:S(2)}, u32[]{:S(2)}) async-start(f32[32,65,256]{2,1,0:T(8,128)} %broadcast_in_dim.49), calls=%async_computation.1 | async-start | bytes 4718592 | tf_op jit(solution)/shard_map/all_to_all | solution.py:35
  148.9 76.0 %copy-start = (f32[256]{0:T(256)S(1)}, f32[256]{0:T(256)}, u32[]{:S(2)}) copy-start(f32[256]{0:T(256)} %param.11) | copy-start | bytes 3076
  148.9 85.9 %copy-start.1 = (f32[256]{0:T(256)S(1)}, f32[256]{0:T(256)}, u32[]{:S(2)}) copy-start(f32[256]{0:T(256)} %param.10) | copy-start | bytes 3076
  163.2 54.6 %all-to-all-start.2 = ((f32[32,1,8192]{2,1,0:T(1,128)}), f32[32,1,8192]{2,1,0:T(1,128)S(1)}, u32[]{:S(2)}, u32[]{:S(2)}) async-start(f32[32,1,8192]{2,1,0:T(1,128)} %broadcast_in_dim.50), calls=%async_computation.2 | async-start | bytes 2097152 | tf_op jit(solution)/shard_map/all_to_all | solution.py:35
  219.1 15.6 %all-to-all-start.3 = ((f32[32,1,256]{2,1,0:T(1,128)}), f32[32,1,256]{2,1,0:T(1,128)S(1)}, u32[]{:S(2)}, u32[]{:S(2)}) async-start(f32[32,1,256]{2,1,0:T(1,128)} %bitcast.5), calls=%async_computation.3 | async-start | bytes 65536 | tf_op jit(solution)/shard_map/all_to_all | solution.py:54
where the time goes:
time: 236 us; the launch traced here: 235 us
  blocking collectives  95.3 us (40%)
  waiting for transfers between devices  45.7 us (19%)
  matrix products  36.4 us (15%)
  other arithmetic  27.1 us (11%)
  starting transfers between devices  22.5 us (10%)
  local copies, waits for them, and re-layouts  4.76 us (2%)
  between operations  3.45 us (1%)
    psum x5, blocking collectives, by_axis_2(): x = lax.psum(x, axis)  44.4 us
    pmax x5, blocking collectives, by_axis(): x = lax.pmax(x, axis)  38.6 us
    all_to_all x3, waiting for transfers between devices, sent_to_all(): return lax.all_to_all(copies, axis, split_axis=0, concat_axis=0, tiled=True)  36.5 us
    dot_general x8, matrix products, block(): lax.dot_general(points, ycols, (((0,), (0,)), ((), ())), precision=lax.Pr...  36.4 us
    all_to_all x3, starting transfers between devices, sent_to_all(): return lax.all_to_all(copies, axis, split_axis=0, concat_axis=0, tiled=True)  16.7 us
    reduce_sum x8, other arithmetic, block(): jnp.sum(jnp.exp(others - new_col[None, :]), 0)  13.5 us
    all_to_all x1, waiting for transfers between devices, sum_at_owner(): pieces = lax.all_to_all(cut_along(x, dim, devices), axis, 0, 0, tiled=True)  9.15 us
    all_to_all x1, blocking collectives, sent_to_all(): return lax.all_to_all(copies, axis, split_axis=0, concat_axis=0, tiled=True)  6.21 us
  transfers between devices with their start and end apart: 4, of which 3 were waited for; matrix products, arithmetic and copies ran while one was open for 1% of the time, Pallas kernels for 0%

commit v1 on v0

--- a/solution.py
+++ b/solution.py
@@ -20,7 +20,11 @@
 
 def by_axis_2(x, axes):
     for axis in axes:
-        x = lax.psum(x, axis)
+
+        def series_all_make(mine_x):
+            return jnp.sum(jax.lax.all_gather(mine_x, axis), 0)
+
+        x = series_all_make(x)
     return x
 
 

time: 236 us -> 282 us (1.19)
  other arithmetic: 27.1 us -> 50.3 us
  local copies, waits for them, and re-layouts: 4.76 us -> 22.1 us
  matrix products: 36.4 us -> 47.8 us
  blocking collectives: 95.3 us -> 88.7 us
    psum x5 -> x0, blocking collectives: 44.4 us -> none  [by_axis_2(): x = lax.psum(x, axis)]
    unnamed x0 -> x5, blocking collectives: none -> 37.8 us
    unnamed x7 -> x42, local copies, waits for them, and re-layouts: 0.13 us -> 17.4 us
    reduce_sum x8, other arithmetic: 13.5 us -> 30.6 us  [block(): jnp.sum(jnp.exp(others - new_col[None, :]), 0)]
    dot_general x8, matrix products: 36.4 us -> 47.8 us  [block(): lax.dot_general(points, ycols, (((0,), (0,)), ((), ())), precision=lax.Pr...]
    reduce_sum x0 -> x10, other arithmetic: none -> 6 us  [series_all_make(): return jnp.sum(jax.lax.all_gather(mine_x, axis), 0)]
  transfers between devices with their start and end apart: 4 -> 4, of which waited for: 3 -> 3; matrix products, arithmetic and copies ran while one was open for 1% -> 9% of each run, Pallas kernels for 0% -> 0%
where the time goes in v1:
time: 282 us; the launch traced here: 281 us
  blocking collectives  88.7 us (31%)
  other arithmetic  50.3 us (18%)
  matrix products  47.8 us (17%)
  waiting for transfers between devices  45.7 us (16%)
  starting transfers between devices  22.5 us (8%)
  local copies, waits for them, and re-layouts  22.1 us (8%)
  between operations  3.57 us (1%)
    dot_general x8, matrix products, block(): lax.dot_general(points, ycols, (((0,), (0,)), ((), ())), precision=lax.Pr...  47.8 us
    pmax x5, blocking collectives, by_axis(): x = lax.pmax(x, axis)  38.6 us
    unnamed x5, blocking collectives  37.8 us
    all_to_all x3, waiting for transfers between devices, sent_to_all(): return lax.all_to_all(copies, axis, split_axis=0, concat_axis=0, tiled=True)  36.5 us
    reduce_sum x8, other arithmetic, block(): jnp.sum(jnp.exp(others - new_col[None, :]), 0)  30.6 us
    unnamed x42, local copies, waits for them, and re-layouts  17.4 us
    all_to_all x3, starting transfers between devices, sent_to_all(): return lax.all_to_all(copies, axis, split_axis=0, concat_axis=0, tiled=True)  16.7 us
    all_to_all x1, waiting for transfers between devices, sum_at_owner(): pieces = lax.all_to_all(cut_along(x, dim, devices), axis, 0, 0, tiled=True)  9.15 us
  transfers between devices with their start and end apart: 4, of which 3 were waited for; matrix products, arithmetic and copies ran while one was open for 9% of the time, Pallas kernels for 0%

profile of v1, /device:TPU:0, one launch (start us, length us, event | category | flops | bytes accessed | tf_op | source)
XLA Modules:
  0.0 281.1 jit_solution(5034064486585965825)
XLA Ops:
  0.6 1.3 reduce_max.63
  1.9 1.3 reduce_max.65
  3.2 5.6 %all-reduce.19 = (f32[]{:T(128)}, f32[]{:T(128)}) all-reduce(f32[]{:T(128)} %reduce_max.63, f32[]{:T(128)} %reduce_max.65), channel_id=1, replica_groups=mesh['grp_0'=2,'grp_1'=2,'mem_0'=2,'mem_1'=4,'mem_2'=4] {'grp_0'}, use_global_device_ids=true, to_apply=%region_11.0 | all-reduce | flops 2 | bytes 16 | tf_op jit(solution)/shard_map/pmax | solution.py:17
  8.8 3.1 %all-reduce.18 = (f32[]{:T(128)}, f32[]{:T(128)}) all-reduce(f32[]{:T(128)} %get-tuple-element.233, f32[]{:T(128)} %get-tuple-element.234), channel_id=1, replica_groups=mesh['grp_0'=2,'grp_1'=2,'mem_0'=2,'mem_1'=4,'mem_2'=4] {'grp_1'}, use_global_device_ids=true, to_apply=%region_12.0 | all-reduce | flops 2 | bytes 16 | tf_op jit(solution)/shard_map/pmax | solution.py:17
  11.8 7.5 %all-reduce.17 = (f32[]{:T(128)}, f32[]{:T(128)}) all-reduce(f32[]{:T(128)} %get-tuple-element.231, f32[]{:T(128)} %get-tuple-element.232), channel_id=1, replica_groups=mesh['grp_0'=2,'grp_1'=2,'mem_0'=2,'mem_1'=4,'mem_2'=4] {'mem_0'}, use_global_device_ids=true, to_apply=%region_13.0 | all-reduce | flops 2 | bytes 16 | tf_op jit(solution)/shard_map/pmax | solution.py:17
  19.3 11.1 %all-reduce.13 = (f32[]{:T(128)}, f32[]{:T(128)}) all-reduce(f32[]{:T(128)} %get-tuple-element.229, f32[]{:T(128)} %get-tuple-element.230), channel_id=1, replica_groups=mesh['grp_0'=2,'grp_1'=2,'mem_0'=2,'mem_1'=4,'mem_2'=4] {'mem_1'}, use_global_device_ids=true, to_apply=%region_14.0 | all-reduce | flops 2 | bytes 16 | tf_op jit(solution)/shard_map/pmax | solution.py:17
  30.4 11.4 %all-reduce.12 = (f32[]{:T(128)}, f32[]{:T(128)}) all-reduce(f32[]{:T(128)} %get-tuple-element.221, f32[]{:T(128)} %get-tuple-element.222), channel_id=1, replica_groups=mesh['grp_0'=2,'grp_1'=2,'mem_0'=2,'mem_1'=4,'mem_2'=4] {'mem_2'}, use_global_device_ids=true, to_apply=%region_15.0 | all-reduce | flops 2 | bytes 16 | tf_op jit(solution)/shard_map/pmax | solution.py:17
  41.8 2.7 exponential_reduce_fusion.2
  44.4 0.8 pad_maximum_fusion
  45.3 0.7 broadcast_in_dim.47
  46.0 3.5 %all-to-all-start = ((f32[4,65,256]{2,1,0:T(8,128)}), f32[4,65,256]{2,1,0:T(8,128)S(1)}, u32[]{:S(2)}, u32[]{:S(2)}) async-start(f32[4,65,256]{2,1,0:T(8,128)} %broadcast_in_dim.47), calls=%async_computation | async-start | bytes 589824 | tf_op jit(solution)/shard_map/all_to_all | solution.py:39
  49.5 0.8 pad_maximum_fusion.1
  50.3 5.5 %all-to-all-done = f32[4,65,256]{2,1,0:T(8,128)S(1)} async-done(((f32[4,65,256]{2,1,0:T(8,128)}), f32[4,65,256]{2,1,0:T(8,128)S(1)}, u32[]{:S(2)}, u32[]{:S(2)}) %all-to-all-start) | async-done | bytes 266272 | tf_op jit(solution)/shard_map/all_to_all | solution.py:39
  55.8 1.6 broadcast_in_dim.49
  57.4 5.8 %all-to-all-start.1 = ((f32[32,65,256]{2,1,0:T(8,128)}), f32[32,65,256]{2,1,0:T(8,128)S(1)}, u32[]{:S(2)}, u32[]{:S(2)}) async-start(f32[32,65,256]{2,1,0:T(8,128)} %broadcast_in_dim.49), calls=%async_computation.1 | async-start | bytes 4718592 | tf_op jit(solution)/shard_map/all_to_all | solution.py:39
  63.5 31.0 %all-to-all-done.1 = f32[32,65,256]{2,1,0:T(8,128)S(1)} async-done(((f32[32,65,256]{2,1,0:T(8,128)}), f32[32,65,256]{2,1,0:T(8,128)S(1)}, u32[]{:S(2)}, u32[]{:S(2)}) %all-to-all-start.1) | async-done | bytes 2129952 | tf_op jit(solution)/shard_map/all_to_all | solution.py:39
  95.2 82.6 %while.20 = (s32[]{:T(128)}, f32[8192]{0:T(1024)S(1)}, f32[8192]{0:T(1024)S(1)}, f32[1024]{0:T(1024)S(1)}, f32[1024]{0:T(1024)S(1)}, /*index=5*/f32[65,1024]{1,0...) while((s32[]{:T(128)}, f32[8192]{0:T(1024)S(1)}, ...), condition=%wide.region_7.0_spmd.clone, body=%wide.region_1.0_spmd.clone.sunk | while | flops 818995456 | bytes 11102434 | solution.py:99
  95.3 6.0 %subtract_reduce_fusion.3 = (f32[128]{0:T(128)S(1)}, f32[8192]{0:T(1024)S(1)}, f32[8192,128]{0,1:T(8,128)}) fusion(f32[8192]{0:T(1024)S(1)} %bitcast.51, f32[128]{0:T(128)S(1)} %dynamic-slice_bitcast_fusion.2, f32[64,8192]{1,0:T(8,128)S(1)} %get-tuple-element.350, f32[65,1024]{1,0:T(8,128)S(1)} %get-tuple-element.348, s32[]{:T(128)S(6)} %select_n.21, ...), kind=kOutput, calls=%fused_computation.5.clone.1 | convolution fusion | flops 812638080 | bytes 6424068 | tf_op jit(solution)/shard_map/while/body/eval_jaxpr/dot_general | solution.py:74
  101.5 3.8 %exponential_reduce_fusion.5 = (f32[128]{0:T(128)S(1)}, f32[8192]{0:T(1024)S(1)}) fusion(f32[8192,128]{0,1:T(8,128)} %get-tuple-element.309, f32[128]{0:T(128)S(1)} %get-tuple-element.311, f32[8192]{0:T(1024)S(1)} %bitcast.52, f32[8192]{0:T(1024)S(1)} %select_maximum_fusion.2, f32[128]{0:T(128)S(1)} %dynamic-slice_bitcast_fusion.2), kind=kLoop, calls=%fused_computation.3.clone.1 | loop fusion | flops 6283136 | bytes 4294144 | tf_op jit(solution)/shard_map/while/body/eval_jaxpr/reduce_sum | solution.py:92
  105.6 6.0 %subtract_reduce_fusion.3 = (f32[128]{0:T(128)S(1)}, f32[8192]{0:T(1024)S(1)}, f32[8192,128]{0,1:T(8,128)}) fusion(f32[8192]{0:T(1024)S(1)} %bitcast.51, f32[128]{0:T(128)S(1)} %dynamic-slice_bitcast_fusion.2, f32[64,8192]{1,0:T(8,128)S(1)} %get-tuple-element.350, f32[65,1024]{1,0:T(8,128)S(1)} %get-tuple-element.348, s32[]{:T(128)S(6)} %select_n.21, ...), kind=kOutput, calls=%fused_computation.5.clone.1 | convolution fusion | flops 812638080 | bytes 6424068 | tf_op jit(solution)/shard_map/while/body/eval_jaxpr/dot_general | solution.py:74
  111.8 3.8 %exponential_reduce_fusion.5 = (f32[128]{0:T(128)S(1)}, f32[8192]{0:T(1024)S(1)}) fusion(f32[8192,128]{0,1:T(8,128)} %get-tuple-element.309, f32[128]{0:T(128)S(1)} %get-tuple-element.311, f32[8192]{0:T(1024)S(1)} %bitcast.52, f32[8192]{0:T(1024)S(1)} %select_maximum_fusion.2, f32[128]{0:T(128)S(1)} %dynamic-slice_bitcast_fusion.2), kind=kLoop, calls=%fused_computation.3.clone.1 | loop fusion | flops 6283136 | bytes 4294144 | tf_op jit(solution)/shard_map/while/body/eval_jaxpr/reduce_sum | solution.py:92
  115.9 6.0 %subtract_reduce_fusion.3 = (f32[128]{0:T(128)S(1)}, f32[8192]{0:T(1024)S(1)}, f32[8192,128]{0,1:T(8,128)}) fusion(f32[8192]{0:T(1024)S(1)} %bitcast.51, f32[128]{0:T(128)S(1)} %dynamic-slice_bitcast_fusion.2, f32[64,8192]{1,0:T(8,128)S(1)} %get-tuple-element.350, f32[65,1024]{1,0:T(8,128)S(1)} %get-tuple-element.348, s32[]{:T(128)S(6)} %select_n.21, ...), kind=kOutput, calls=%fused_computation.5.clone.1 | convolution fusion | flops 812638080 | bytes 6424068 | tf_op jit(solution)/shard_map/while/body/eval_jaxpr/dot_general | solution.py:74
  122.1 3.8 %exponential_reduce_fusion.5 = (f32[128]{0:T(128)S(1)}, f32[8192]{0:T(1024)S(1)}) fusion(f32[8192,128]{0,1:T(8,128)} %get-tuple-element.309, f32[128]{0:T(128)S(1)} %get-tuple-element.311, f32[8192]{0:T(1024)S(1)} %bitcast.52, f32[8192]{0:T(1024)S(1)} %select_maximum_fusion.2, f32[128]{0:T(128)S(1)} %dynamic-slice_bitcast_fusion.2), kind=kLoop, calls=%fused_computation.3.clone.1 | loop fusion | flops 6283136 | bytes 4294144 | tf_op jit(solution)/shard_map/while/body/eval_jaxpr/reduce_sum | solution.py:92
  126.3 6.0 %subtract_reduce_fusion.3 = (f32[128]{0:T(128)S(1)}, f32[8192]{0:T(1024)S(1)}, f32[8192,128]{0,1:T(8,128)}) fusion(f32[8192]{0:T(1024)S(1)} %bitcast.51, f32[128]{0:T(128)S(1)} %dynamic-slice_bitcast_fusion.2, f32[64,8192]{1,0:T(8,128)S(1)} %get-tuple-element.350, f32[65,1024]{1,0:T(8,128)S(1)} %get-tuple-element.348, s32[]{:T(128)S(6)} %select_n.21, ...), kind=kOutput, calls=%fused_computation.5.clone.1 | convolution fusion | flops 812638080 | bytes 6424068 | tf_op jit(solution)/shard_map/while/body/eval_jaxpr/dot_general | solution.py:74
  132.5 3.8 %exponential_reduce_fusion.5 = (f32[128]{0:T(128)S(1)}, f32[8192]{0:T(1024)S(1)}) fusion(f32[8192,128]{0,1:T(8,128)} %get-tuple-element.309, f32[128]{0:T(128)S(1)} %get-tuple-element.311, f32[8192]{0:T(1024)S(1)} %bitcast.52, f32[8192]{0:T(1024)S(1)} %select_maximum_fusion.2, f32[128]{0:T(128)S(1)} %dynamic-slice_bitcast_fusion.2), kind=kLoop, calls=%fused_computation.3.clone.1 | loop fusion | flops 6283136 | bytes 4294144 | tf_op jit(solution)/shard_map/while/body/eval_jaxpr/reduce_sum | solution.py:92
  136.6 6.0 %subtract_reduce_fusion.3 = (f32[128]{0:T(128)S(1)}, f32[8192]{0:T(1024)S(1)}, f32[8192,128]{0,1:T(8,128)}) fusion(f32[8192]{0:T(1024)S(1)} %bitcast.51, f32[128]{0:T(128)S(1)} %dynamic-slice_bitcast_fusion.2, f32[64,8192]{1,0:T(8,128)S(1)} %get-tuple-element.350, f32[65,1024]{1,0:T(8,128)S(1)} %get-tuple-element.348, s32[]{:T(128)S(6)} %select_n.21, ...), kind=kOutput, calls=%fused_computation.5.clone.1 | convolution fusion | flops 812638080 | bytes 6424068 | tf_op jit(solution)/shard_map/while/body/eval_jaxpr/dot_general | solution.py:74
  142.8 3.8 %exponential_reduce_fusion.5 = (f32[128]{0:T(128)S(1)}, f32[8192]{0:T(1024)S(1)}) fusion(f32[8192,128]{0,1:T(8,128)} %get-tuple-element.309, f32[128]{0:T(128)S(1)} %get-tuple-element.311, f32[8192]{0:T(1024)S(1)} %bitcast.52, f32[8192]{0:T(1024)S(1)} %select_maximum_fusion.2, f32[128]{0:T(128)S(1)} %dynamic-slice_bitcast_fusion.2), kind=kLoop, calls=%fused_computation.3.clone.1 | loop fusion | flops 6283136 | bytes 4294144 | tf_op jit(solution)/shard_map/while/body/eval_jaxpr/reduce_sum | solution.py:92
  146.9 6.0 %subtract_reduce_fusion.3 = (f32[128]{0:T(128)S(1)}, f32[8192]{0:T(1024)S(1)}, f32[8192,128]{0,1:T(8,128)}) fusion(f32[8192]{0:T(1024)S(1)} %bitcast.51, f32[128]{0:T(128)S(1)} %dynamic-slice_bitcast_fusion.2, f32[64,8192]{1,0:T(8,128)S(1)} %get-tuple-element.350, f32[65,1024]{1,0:T(8,128)S(1)} %get-tuple-element.348, s32[]{:T(128)S(6)} %select_n.21, ...), kind=kOutput, calls=%fused_computation.5.clone.1 | convolution fusion | flops 812638080 | bytes 6424068 | tf_op jit(solution)/shard_map/while/body/eval_jaxpr/dot_general | solution.py:74
  153.1 3.8 %exponential_reduce_fusion.5 = (f32[128]{0:T(128)S(1)}, f32[8192]{0:T(1024)S(1)}) fusion(f32[8192,128]{0,1:T(8,128)} %get-tuple-element.309, f32[128]{0:T(128)S(1)} %get-tuple-element.311, f32[8192]{0:T(1024)S(1)} %bitcast.52, f32[8192]{0:T(1024)S(1)} %select_maximum_fusion.2, f32[128]{0:T(128)S(1)} %dynamic-slice_bitcast_fusion.2), kind=kLoop, calls=%fused_computation.3.clone.1 | loop fusion | flops 6283136 | bytes 4294144 | tf_op jit(solution)/shard_map/while/body/eval_jaxpr/reduce_sum | solution.py:92
  157.3 6.0 %subtract_reduce_fusion.3 = (f32[128]{0:T(128)S(1)}, f32[8192]{0:T(1024)S(1)}, f32[8192,128]{0,1:T(8,128)}) fusion(f32[8192]{0:T(1024)S(1)} %bitcast.51, f32[128]{0:T(128)S(1)} %dynamic-slice_bitcast_fusion.2, f32[64,8192]{1,0:T(8,128)S(1)} %get-tuple-element.350, f32[65,1024]{1,0:T(8,128)S(1)} %get-tuple-element.348, s32[]{:T(128)S(6)} %select_n.21, ...), kind=kOutput, calls=%fused_computation.5.clone.1 | convolution fusion | flops 812638080 | bytes 6424068 | tf_op jit(solution)/shard_map/while/body/eval_jaxpr/dot_general | solution.py:74
  163.4 3.8 %exponential_reduce_fusion.5 = (f32[128]{0:T(128)S(1)}, f32[8192]{0:T(1024)S(1)}) fusion(f32[8192,128]{0,1:T(8,128)} %get-tuple-element.309, f32[128]{0:T(128)S(1)} %get-tuple-element.311, f32[8192]{0:T(1024)S(1)} %bitcast.52, f32[8192]{0:T(1024)S(1)} %select_maximum_fusion.2, f32[128]{0:T(128)S(1)} %dynamic-slice_bitcast_fusion.2), kind=kLoop, calls=%fused_computation.3.clone.1 | loop fusion | flops 6283136 | bytes 4294144 | tf_op jit(solution)/shard_map/while/body/eval_jaxpr/reduce_sum | solution.py:92
  167.6 6.0 %subtract_reduce_fusion.3 = (f32[128]{0:T(128)S(1)}, f32[8192]{0:T(1024)S(1)}, f32[8192,128]{0,1:T(8,128)}) fusion(f32[8192]{0:T(1024)S(1)} %bitcast.51, f32[128]{0:T(128)S(1)} %dynamic-slice_bitcast_fusion.2, f32[64,8192]{1,0:T(8,128)S(1)} %get-tuple-element.350, f32[65,1024]{1,0:T(8,128)S(1)} %get-tuple-element.348, s32[]{:T(128)S(6)} %select_n.21, ...), kind=kOutput, calls=%fused_computation.5.clone.1 | convolution fusion | flops 812638080 | bytes 6424068 | tf_op jit(solution)/shard_map/while/body/eval_jaxpr/dot_general | solution.py:74
  173.8 3.8 %exponential_reduce_fusion.5 = (f32[128]{0:T(128)S(1)}, f32[8192]{0:T(1024)S(1)}) fusion(f32[8192,128]{0,1:T(8,128)} %get-tuple-element.309, f32[128]{0:T(128)S(1)} %get-tuple-element.311, f32[8192]{0:T(1024)S(1)} %bitcast.52, f32[8192]{0:T(1024)S(1)} %select_maximum_fusion.2, f32[128]{0:T(128)S(1)} %dynamic-slice_bitcast_fusion.2), kind=kLoop, calls=%fused_computation.3.clone.1 | loop fusion | flops 6283136 | bytes 4294144 | tf_op jit(solution)/shard_map/while/body/eval_jaxpr/reduce_sum | solution.py:92
  177.9 6.2 %all_to_all.40 = f32[4,1,1024]{2,1,0:T(1,128)S(1)} all-to-all(f32[4,1,1024]{2,1,0:T(1,128)S(1)} %broadcast_in_dim.51), channel_id=1, replica_groups=mesh['grp_0'=2,'grp_1'=2,'mem_0'=2,'mem_1'=4,'mem_2'=4] {'grp_0','grp_1'}, dimensions={0} | all-to-all | bytes 32768 | tf_op jit(solution)/shard_map/all_to_all | solution.py:39
  184.1 6.1 %all_to_all.41 = f32[4,1,256]{2,1,0:T(1,128)S(1)} all-to-all(f32[4,1,256]{2,1,0:T(1,128)S(1)} %bitcast.57), channel_id=1, replica_groups=mesh['grp_0'=2,'grp_1'=2,'mem_0'=2,'mem_1'=4,'mem_2'=4] {'grp_0','grp_1'}, dimensions={0} | all-to-all | bytes 8192 | tf_op jit(solution)/shard_map/all_to_all | solution.py:58
  190.3 1.9 broadcast_in_dim.50
  192.2 7.5 %all-to-all-start.2 = ((f32[32,1,8192]{2,1,0:T(1,128)}), f32[32,1,8192]{2,1,0:T(1,128)S(1)}, u32[]{:S(2)}, u32[]{:S(2)}) async-start(f32[32,1,8192]{2,1,0:T(1,128)} %broadcast_in_dim.50), calls=%async_computation.2 | async-start | bytes 2097152 | tf_op jit(solution)/shard_map/all_to_all | solution.py:39
  200.3 1.4 dynamic-update-slice
  201.7 1.4 dynamic-update-slice.5
  203.1 5.3 %all-reduce.16 = (f32[2]{0:T(128)S(1)}, f32[2]{0:T(128)S(1)}) all-reduce(f32[2]{0:T(128)S(1)} %dynamic-update-slice, f32[2]{0:T(128)S(1)} %dynamic-update-slice.5), channel_id=1, replica_groups=mesh['grp_0'=2,'grp_1'=2,'mem_0'=2,'mem_1'=4,'mem_2'=4] {'grp_0'}, use_global_device_ids=true, to_apply=%add | all-reduce | flops 4 | bytes 32
  208.3 0.7 dynamic-slice.1
  210.2 1.4 dynamic-update-slice.1
  211.6 1.4 dynamic-update-slice.6
  213.0 2.4 all-reduce.15
  215.4 0.7 dynamic-slice.2
  217.3 1.4 dynamic-update-slice.2
  218.8 1.4 dynamic-update-slice.7
  220.1 6.4 %all-reduce.14 = (f32[2]{0:T(128)S(1)}, f32[2]{0:T(128)S(1)}) all-reduce(f32[2]{0:T(128)S(1)} %dynamic-update-slice.2, f32[2]{0:T(128)S(1)} %dynamic-update-slice.7), channel_id=1, replica_groups=mesh['grp_0'=2,'grp_1'=2,'mem_0'=2,'mem_1'=4,'mem_2'=4] {'mem_0'}, use_global_device_ids=true, to_apply=%add.2 | all-reduce | flops 4 | bytes 32
  226.5 0.7 dynamic-slice.3
  228.4 1.4 dynamic-update-slice.3
  229.8 1.4 dynamic-update-slice.8
  231.2 13.5 %all-reduce.11 = (f32[4]{0:T(128)S(1)}, f32[4]{0:T(128)S(1)}) all-reduce(f32[4]{0:T(128)S(1)} %dynamic-update-slice.3, f32[4]{0:T(128)S(1)} %dynamic-update-slice.8), channel_id=1, replica_groups=mesh['grp_0'=2,'grp_1'=2,'mem_0'=2,'mem_1'=4,'mem_2'=4] {'mem_1'}, use_global_device_ids=true, to_apply=%add.3 | all-reduce | flops 8 | bytes 64
  244.7 0.7 dynamic-slice.4
  246.5 1.4 dynamic-update-slice.4
  248.0 1.4 dynamic-update-slice.9
  249.3 10.2 %all-reduce.10 = (f32[4]{0:T(128)S(1)}, f32[4]{0:T(128)S(1)}) all-reduce(f32[4]{0:T(128)S(1)} %dynamic-update-slice.4, f32[4]{0:T(128)S(1)} %dynamic-update-slice.9), channel_id=1, replica_groups=mesh['grp_0'=2,'grp_1'=2,'mem_0'=2,'mem_1'=4,'mem_2'=4] {'mem_2'}, use_global_device_ids=true, to_apply=%add.4 | all-reduce | flops 8 | bytes 64
  259.5 0.6 reduce_sum.188
  261.5 0.6 reduce_sum.181
  263.4 0.7 reduce_max.62
  264.1 0.6 exponential_multiply_fusion
  264.8 5.8 %all-to-all-start.3 = ((f32[32,1,256]{2,1,0:T(1,128)}), f32[32,1,256]{2,1,0:T(1,128)S(1)}, u32[]{:S(2)}, u32[]{:S(2)}) async-start(f32[32,1,256]{2,1,0:T(1,128)} %bitcast.5), calls=%async_computation.3 | async-start | bytes 65536 | tf_op jit(solution)/shard_map/all_to_all | solution.py:58
  270.6 0.6 add_multiply_fusion
  271.2 9.2 %all-to-all-done.3 = f32[32,1,256]{2,1,0:T(1,128)S(1)} async-done(((f32[32,1,256]{2,1,0:T(1,128)}), f32[32,1,256]{2,1,0:T(1,128)S(1)}, u32[]{:S(2)}, u32[]{:S(2)}) %all-to-all-start.3) | async-done | bytes 32800 | tf_op jit(solution)/shard_map/all_to_all | solution.py:58
  280.4 0.6 add_multiply_fusion.1
  (131 shorter events, 10.1 us)
Async XLA Ops:
  46.0 9.8 %all-to-all-start = ((f32[4,65,256]{2,1,0:T(8,128)}), f32[4,65,256]{2,1,0:T(8,128)S(1)}, u32[]{:S(2)}, u32[]{:S(2)}) async-start(f32[4,65,256]{2,1,0:T(8,128)} %broadcast_in_dim.47), calls=%async_computation | async-start | bytes 589824 | tf_op jit(solution)/shard_map/all_to_all | solution.py:39
  57.4 37.1 %all-to-all-start.1 = ((f32[32,65,256]{2,1,0:T(8,128)}), f32[32,65,256]{2,1,0:T(8,128)S(1)}, u32[]{:S(2)}, u32[]{:S(2)}) async-start(f32[32,65,256]{2,1,0:T(8,128)} %broadcast_in_dim.49), calls=%async_computation.1 | async-start | bytes 4718592 | tf_op jit(solution)/shard_map/all_to_all | solution.py:39
  95.2 104.5 %copy-start.6 = (u32[128]{0:T(128)S(1)}, u32[128]{0:T(128)}, u32[]{:S(2)}) copy-start(u32[128]{0:T(128)} %constant.108) | copy-start | bytes 1540
  95.2 113.2 %copy-start.5 = (u32[128]{0:T(128)S(1)}, u32[128]{0:T(128)}, u32[]{:S(2)}) copy-start(u32[128]{0:T(128)} %constant.113) | copy-start | bytes 1540
  95.2 120.3 %copy-start.4 = (u32[128]{0:T(128)S(1)}, u32[128]{0:T(128)}, u32[]{:S(2)}) copy-start(u32[128]{0:T(128)} %constant.118) | copy-start | bytes 1540
  95.2 131.3 %copy-start.3 = (u32[128]{0:T(128)S(1)}, u32[128]{0:T(128)}, u32[]{:S(2)}) copy-start(u32[128]{0:T(128)} %constant.123) | copy-start | bytes 1540
  95.2 149.5 %copy-start.2 = (u32[128]{0:T(128)S(1)}, u32[128]{0:T(128)}, u32[]{:S(2)}) copy-start(u32[128]{0:T(128)} %constant.128) | copy-start | bytes 1540
  177.8 92.7 %copy-start = (f32[256]{0:T(256)S(1)}, f32[256]{0:T(256)}, u32[]{:S(2)}) copy-start(f32[256]{0:T(256)} %param.11) | copy-start | bytes 3076
  177.9 102.6 %copy-start.1 = (f32[256]{0:T(256)S(1)}, f32[256]{0:T(256)}, u32[]{:S(2)}) copy-start(f32[256]{0:T(256)} %param.10) | copy-start | bytes 3076
  192.2 71.2 %all-to-all-start.2 = ((f32[32,1,8192]{2,1,0:T(1,128)}), f32[32,1,8192]{2,1,0:T(1,128)S(1)}, u32[]{:S(2)}, u32[]{:S(2)}) async-start(f32[32,1,8192]{2,1,0:T(1,128)} %broadcast_in_dim.50), calls=%async_computation.2 | async-start | bytes 2097152 | tf_op jit(solution)/shard_map/all_to_all | solution.py:39
  264.8 15.6 %all-to-all-start.3 = ((f32[32,1,256]{2,1,0:T(1,128)}), f32[32,1,256]{2,1,0:T(1,128)S(1)}, u32[]{:S(2)}, u32[]{:S(2)}) async-start(f32[32,1,256]{2,1,0:T(1,128)} %bitcast.5), calls=%async_computation.3 | async-start | bytes 65536 | tf_op jit(solution)/shard_map/all_to_all | solution.py:58
